TPU v7x, 32 devices: a whole 2x2x4 slice. The times are simulated.
32 devices in a mesh: seq: 8 (over z, y), ctx: 4 (over x, core).
Axes of the slice: x: 2, y: 2, z: 4, core: 2. Of those that a mesh axis runs over, the one named last changes fastest.
Arguments:
- hidden_in: bfloat16 [8, 512, 1024], P('seq', 'ctx'), may hold values from -6 to 6
- positions: int32 [8, 512], P('seq', 'ctx'), may hold values from 0 to 499, as said below
- norm1_gain: float32 [1024], replicated, may hold values from 0.5 to 1.5
- w_query: bfloat16 [1024, 2048], P(('seq', 'ctx')), may hold values from -0.1875 to 0.1875
- key_weight_matrix: bfloat16 [1024, 1024], P(('seq', 'ctx')), may hold values from -0.1875 to 0.1875
- value_weight_matrix: bfloat16 [1024, 1024], P(('seq', 'ctx')), may hold values from -0.1875 to 0.1875
- query_gain: float32 [128], replicated, may hold values from 0.8 to 6
- key_gain: float32 [128], replicated, may hold values from 0.8 to 6
- w_out: bfloat16 [1024, 2048], P(('seq', 'ctx')), may hold values from -0.75 to 0.75
- norm2_gain: float32 [1024], replicated, may hold values from 0.5 to 1.5
- w_gate: bfloat16 [1024, 3072], P(('seq', 'ctx')), may hold values from -0.1875 to 0.1875
- w_up: bfloat16 [1024, 3072], P(('seq', 'ctx')), may hold values from -0.1875 to 0.1875
- w_down: bfloat16 [1024, 3072], P(('seq', 'ctx')), may hold values from -0.109375 to 0.109375
- cotangent: bfloat16 [8, 512, 1024], P('seq', 'ctx'), may hold values from -6 to 6
Outputs:
- out_hidden: bfloat16 [8, 512, 1024], P('seq', 'ctx')
- grad_hidden: bfloat16 [8, 512, 1024], P('seq', 'ctx')
- grad_query: float32 [1024, 2048], P(('seq', 'ctx'))
- grad_key: float32 [1024, 1024], P(('seq', 'ctx'))
- grad_value: float32 [1024, 1024], P(('seq', 'ctx'))
- grad_out: float32 [1024, 2048], P(('seq', 'ctx'))
- grad_gate: float32 [1024, 3072], P(('seq', 'ctx'))
- grad_up: float32 [1024, 3072], P(('seq', 'ctx'))
- grad_down: float32 [1024, 3072], P(('seq', 'ctx'))
- grad_norm1: float32 [1024], replicated
- grad_norm2: float32 [1024], replicated
- grad_query_gain: float32 [128], replicated
- grad_key_gain: float32 [128], replicated
Inputs may be any that keep to these rules, and one draw needn't show every extreme that they name: In each sequence positions are 0 at the first token and rise by one from token to token, except at the first token of a document, where they return to 0.
All inputs are finite; a program needn't handle non-finite values.
Results may differ from a plain program's by a relative error of at most 0.04.
The roundings to bfloat16 on the way count: a program that leaves them out, or rounds other values in their place, can miss the bound.
Values may be sent and summed in bfloat16 or wider, within the bound.
No kernel may reach another device: no remote copies, remote signals or barrier semaphores. Data moves between devices by JAX's collectives and lax.ppermute only.
A program may use at most 384 MiB of HBM per device.

v0:
```python
import jax
import jax.numpy as jnp
from jax import lax
from jax.sharding import PartitionSpec as P

NORM_EPSILON = 1e-06
ROPE_THETA = 1000000.0


def rope_tables(position_ids, head_width):
    half_width = head_width // 2
    inverse = ROPE_THETA ** (-(2.0 / head_width) * jnp.arange(half_width, dtype=jnp.float32))
    angles = position_ids.astype(jnp.float32)[:, None] * inverse[None, :]
    return (jnp.cos(angles), jnp.sin(angles))


def rotate(vectors, cosine, sine):
    half_width = vectors.shape[-1] // 2
    first = vectors[..., :half_width]
    second = vectors[..., half_width:]
    cos_rows = cosine[:, None, :]
    sin_rows = sine[:, None, :]
    return jnp.concatenate(
        (first * cos_rows - second * sin_rows, second * cos_rows + first * sin_rows), -1
    )


def rotate_back(grads, cosine, sine):
    half_width = grads.shape[-1] // 2
    first = grads[..., :half_width]
    second = grads[..., half_width:]
    cos_rows = cosine[:, None, :]
    sin_rows = sine[:, None, :]
    return jnp.concatenate(
        (first * cos_rows + second * sin_rows, second * cos_rows - first * sin_rows), -1
    )


def unit_rows(vectors):
    factor = lax.rsqrt(jnp.mean(vectors * vectors, -1, keepdims=True) + NORM_EPSILON)
    return (factor, vectors * factor)


def unit_back(grad_unit, factor, unit):
    return factor * (grad_unit - unit * jnp.mean(grad_unit * unit, -1, keepdims=True))


def outer_rows(left, right):
    return jnp.einsum("tj,tc->jc", left, right, preferred_element_type=jnp.float32)


def shards(
    hidden_in,
    positions,
    norm1_gain,
    w_query,
    key_weight_matrix,
    value_weight_matrix,
    query_gain,
    key_gain,
    w_out,
    norm2_gain,
    w_gate,
    w_up,
    w_down,
    cotangent,
):
    row_count = hidden_in.shape[1]
    head_width = query_gain.shape[0]
    query_columns = w_query.shape[1]
    key_value_columns = key_weight_matrix.shape[1]
    kv_heads = key_value_columns // head_width
    query_group_count = query_columns // key_value_columns
    attn_width = query_columns + 2 * key_value_columns + query_columns
    inputs = hidden_in[0].astype(jnp.float32)
    position_ids = positions[0]
    factor1, unit1 = unit_rows(inputs)
    normed1 = (unit1 * norm1_gain).astype(jnp.bfloat16)
    w_joint = jnp.concatenate((w_query, key_weight_matrix, value_weight_matrix), 1)
    joint_full, out_full = (
        lax.all_gather(w_joint, ("seq", "ctx"), axis=0, tiled=True),
        lax.all_gather(w_out, ("seq", "ctx"), axis=0, tiled=True),
    )
    projected_output = jnp.dot(normed1, joint_full, preferred_element_type=jnp.float32)
    query_raw = projected_output[:, :query_columns].reshape(
        row_count, query_columns // head_width, head_width
    )
    unrotated_key = projected_output[:, query_columns : query_columns + key_value_columns].reshape(
        row_count, kv_heads, head_width
    )
    unprojected_value = projected_output[:, query_columns + key_value_columns :].reshape(
        row_count, kv_heads, head_width
    )
    query_factor, query_unit = unit_rows(query_raw)
    key_factor, key_unit = unit_rows(unrotated_key)
    cosine, sine = rope_tables(position_ids, head_width)
    rotated_query = rotate(query_unit * query_gain, cosine, sine).astype(jnp.bfloat16)
    key_rot = rotate(key_unit * key_gain, cosine, sine).astype(jnp.bfloat16)
    query_head_rows = rotated_query.reshape(
        row_count, kv_heads, query_group_count, head_width
    ).transpose(1, 2, 0, 3)
    own_pair = jnp.stack((key_rot, unprojected_value.astype(jnp.bfloat16)))
    cycle_size = lax.axis_size("ctx")
    my_block = lax.axis_index("ctx")
    offsets = jnp.arange(row_count, dtype=jnp.int32)
    query_index = my_block * row_count + offsets
    doc_begin = query_index - position_ids
    score_scale = head_width ** (-0.5)

    def visible(count):
        key_index = jnp.arange(count, dtype=jnp.int32)
        return (key_index[None, :] <= query_index[:, None]) & (
            key_index[None, :] >= doc_begin[:, None]
        )

    def block_scores(key_value_couple, key_mask):
        scores = score_scale * jnp.einsum(
            "ekla,xea->eklx",
            query_head_rows,
            key_value_couple[0],
            preferred_element_type=jnp.float32,
        )
        return jnp.where(key_mask[None, None], scores, -jnp.inf)

    state = (
        jnp.full((kv_heads, query_group_count, row_count), -jnp.inf, jnp.float32),
        jnp.zeros((kv_heads, query_group_count, row_count), jnp.float32),
        jnp.zeros((kv_heads, query_group_count, row_count, head_width), jnp.float32),
    )
    key_value_couple = lax.all_gather(own_pair, "ctx", axis=1, tiled=True)
    key_mask = visible(key_value_couple.shape[1])

    def attend(current):
        highest, totals, accum = current
        scores = block_scores(key_value_couple, key_mask)
        new_high = jnp.max(scores, -1)
        decay = jnp.exp(highest - new_high)
        weights = jnp.exp(scores - new_high[..., None])
        totals = totals * decay + jnp.sum(weights, -1)
        accum = accum * decay[..., None] + jnp.einsum(
            "emaj,jep->emap",
            weights.astype(jnp.bfloat16),
            key_value_couple[1],
            preferred_element_type=jnp.float32,
        )
        return (new_high, totals, accum)

    highest, totals, accum = lax.cond(jnp.any(key_mask), attend, lambda current: current, state)
    log_total = highest + jnp.log(totals)
    attn_heads = (accum / totals[..., None]).astype(jnp.bfloat16)
    attention_row_block = attn_heads.transpose(2, 0, 1, 3).reshape(row_count, query_columns)
    attn_out = jnp.einsum(
        "tc,jc->tj", attention_row_block, out_full, preferred_element_type=jnp.float32
    )
    residual = inputs + attn_out
    factor2, unit2 = unit_rows(residual)
    normed2 = (unit2 * norm2_gain).astype(jnp.bfloat16)
    gate_full, up_full, down_full = (
        lax.all_gather(w_gate, ("seq", "ctx"), axis=0, tiled=True),
        lax.all_gather(w_up, ("seq", "ctx"), axis=0, tiled=True),
        lax.all_gather(w_down, ("seq", "ctx"), axis=0, tiled=True),
    )
    gate = jnp.dot(normed2, gate_full, preferred_element_type=jnp.float32)
    upward = jnp.dot(normed2, up_full, preferred_element_type=jnp.float32)
    sigmoid = jax.nn.sigmoid(gate)
    activation = gate * sigmoid
    hidden_units = (activation * upward).astype(jnp.bfloat16)
    mlp_out = jnp.einsum("tf,jf->tj", hidden_units, down_full, preferred_element_type=jnp.float32)
    out_hidden = (residual + mlp_out).astype(jnp.bfloat16)
    grad_out_b = cotangent[0]
    grad_hidden = jnp.dot(grad_out_b, down_full, preferred_element_type=jnp.float32)
    grad_gate = (grad_hidden * upward * sigmoid * (1.0 + gate * (1.0 - sigmoid))).astype(
        jnp.bfloat16
    )
    grad_up = (grad_hidden * activation).astype(jnp.bfloat16)
    grad_normed2 = jnp.einsum(
        "tf,jf->tj", grad_gate, gate_full, preferred_element_type=jnp.float32
    ) + jnp.einsum("tf,jf->tj", grad_up, up_full, preferred_element_type=jnp.float32)
    gain2_local = jnp.sum(grad_normed2 * unit2, 0)
    grad_residual = grad_out_b.astype(jnp.float32) + unit_back(
        grad_normed2 * norm2_gain, factor2, unit2
    )
    grad_residual_b = grad_residual.astype(jnp.bfloat16)
    grad_attn = jnp.dot(grad_residual_b, out_full, preferred_element_type=jnp.float32)
    attention_gradient_backward = grad_attn.astype(jnp.bfloat16)
    head_gradient = attention_gradient_backward.reshape(
        row_count, kv_heads, query_group_count, head_width
    ).transpose(1, 2, 0, 3)
    delta_rows = jnp.sum(head_gradient.astype(jnp.float32) * attn_heads.astype(jnp.float32), -1)
    grads_full = jnp.zeros((2, row_count * cycle_size, kv_heads, head_width), jnp.float32)
    grad_q_acc = jnp.zeros((kv_heads, query_group_count, row_count, head_width), jnp.float32)
    current = (grads_full, grad_q_acc)
    backward_key_value_couple = lax.all_gather(own_pair, "ctx", axis=1, tiled=True)
    piece_rows = backward_key_value_couple.shape[1]
    backward_key_mask = visible(piece_rows)

    def attend_back(inner):
        scores = block_scores(backward_key_value_couple, backward_key_mask)
        probs = jnp.exp(scores - log_total[..., None])
        probability_backward = probs.astype(jnp.bfloat16)
        grad_probs = jnp.einsum(
            "ekla,xea->eklx",
            head_gradient,
            backward_key_value_couple[1],
            preferred_element_type=jnp.float32,
        )
        score_gradient = (probs * (grad_probs - delta_rows[..., None])).astype(jnp.bfloat16)
        grad_q_acc = score_scale * jnp.einsum(
            "emaj,jep->emap",
            score_gradient,
            backward_key_value_couple[0],
            preferred_element_type=jnp.float32,
        )
        grad_keys = score_scale * jnp.einsum(
            "kejx,kejy->xky", score_gradient, query_head_rows, preferred_element_type=jnp.float32
        )
        grad_values = jnp.einsum(
            "kejx,kejy->xky",
            probability_backward,
            head_gradient,
            preferred_element_type=jnp.float32,
        )
        grads_full = jnp.stack((grad_keys, grad_values))
        return (grads_full, grad_q_acc)

    grads_full, grad_q_acc = lax.cond(
        jnp.any(backward_key_mask), attend_back, lambda inner: inner, current
    )
    grads_kv = lax.psum_scatter(
        grads_full.astype(jnp.bfloat16), "ctx", scatter_dimension=1, tiled=True
    ).astype(jnp.float32)
    grad_query = rotate_back(
        grad_q_acc.transpose(2, 0, 1, 3).reshape(
            row_count, query_columns // head_width, head_width
        ),
        cosine,
        sine,
    )
    grad_key = rotate_back(grads_kv[0], cosine, sine)
    qgain_local = jnp.sum(grad_query * query_unit, (0, 1))
    kgain_local = jnp.sum(grad_key * key_unit, (0, 1))
    grad_query_raw = unit_back(grad_query * query_gain, query_factor, query_unit)
    grad_key_raw = unit_back(grad_key * key_gain, key_factor, key_unit)
    grad_joint = jnp.concatenate(
        (
            grad_query_raw.reshape(row_count, query_columns),
            grad_key_raw.reshape(row_count, key_value_columns),
            grads_kv[1].reshape(row_count, key_value_columns),
        ),
        1,
    ).astype(jnp.bfloat16)
    grad_normed1 = jnp.einsum(
        "tc,jc->tj", grad_joint, joint_full, preferred_element_type=jnp.float32
    )
    gain1_local = jnp.sum(grad_normed1 * unit1, 0)
    grad_inputs = (grad_residual + unit_back(grad_normed1 * norm1_gain, factor1, unit1)).astype(
        jnp.bfloat16
    )
    joined = lax.psum_scatter(
        jnp.concatenate(
            (
                jnp.concatenate(
                    (
                        outer_rows(normed1, grad_joint),
                        outer_rows(grad_residual_b, attention_row_block),
                    ),
                    1,
                ),
                jnp.concatenate(
                    (
                        outer_rows(normed2, grad_gate),
                        outer_rows(normed2, grad_up),
                        outer_rows(grad_out_b, hidden_units),
                    ),
                    1,
                ),
            ),
            1,
        ),
        ("seq", "ctx"),
        scatter_dimension=0,
        tiled=True,
    )
    attn_grads = joined[:, :attn_width]
    mlp_grads = joined[:, attn_width:]
    gain_totals = lax.psum((gain1_local, gain2_local, qgain_local, kgain_local), ("seq", "ctx"))
    hidden_width = w_gate.shape[1]
    return (
        out_hidden[None],
        grad_inputs[None],
        attn_grads[:, :query_columns],
        attn_grads[:, query_columns : query_columns + key_value_columns],
        attn_grads[:, query_columns + key_value_columns : query_columns + 2 * key_value_columns],
        attn_grads[:, query_columns + 2 * key_value_columns :],
        mlp_grads[:, :hidden_width],
        mlp_grads[:, hidden_width : 2 * hidden_width],
        mlp_grads[:, 2 * hidden_width :],
        gain_totals[0],
        gain_totals[1],
        gain_totals[2],
        gain_totals[3],
    )


def solution(mesh):
    placed = (
        P("seq", "ctx", None),
        P("seq", "ctx"),
        P(),
        P(("seq", "ctx"), None),
        P(("seq", "ctx"), None),
        P(("seq", "ctx"), None),
        P(),
        P(),
        P(("seq", "ctx"), None),
        P(),
        P(("seq", "ctx"), None),
        P(("seq", "ctx"), None),
        P(("seq", "ctx"), None),
        P("seq", "ctx", None),
    )
    return jax.shard_map(
        shards,
        mesh=mesh,
        in_specs=placed,
        out_specs=(
            P("seq", "ctx", None),
            P("seq", "ctx", None),
            P(("seq", "ctx"), None),
            P(("seq", "ctx"), None),
            P(("seq", "ctx"), None),
            P(("seq", "ctx"), None),
            P(("seq", "ctx"), None),
            P(("seq", "ctx"), None),
            P(("seq", "ctx"), None),
            P(),
            P(),
            P(),
            P(),
        ),
        check_vma=False,
    )
```

profile of v0, /device:TPU:0, one launch (start us, length us, event | category | flops | bytes accessed | tf_op | source)
XLA Modules:
  0.0 1033.1 jit_solution(10262787991396275115)
XLA Ops:
  11.1 80.1 %all-gather.7.cloned.1.call-done = bf16[1024,4096]{1,0:T(8,128)(2,1)} async-done(((bf16[32,4096]{1,0:T(8,128)(2,1)}), bf16[1024,4096]{1,0:T(8,128)(2,1)}) %all-gather.7.cloned.1.call-update) | async-done | bytes 8388624 | tf_op jit(solution)/shard_map/all_gather | solution.py:81
  91.2 4.8 fusion.78
  105.8 13.8 %all-gather.9.cloned.1.call-done = bf16[2,512,8,128]{3,1,2,0:T(8,128)(2,1)} async-done(((bf16[2,128,8,128]{3,1,2,0:T(8,128)(2,1)}), bf16[2,512,8,128]{3,1,2,0:T(8,128)(2,1)}) %all-gather.9.cloned.1.call-update) | async-done | bytes 2097168 | tf_op jit(solution)/shard_map/all_gather | solution.py:130
  119.6 11.9 %conditional.2 = (f32[8,2,128]{2,1,0:T(2,128)}, f32[8,2,128]{2,1,0:T(2,128)S(1)}, f32[8,2,128]{2,1,0:T(2,128)}, f32[8,2,128,128]{2,3,1,0:T(8,128)}) conditional(s32[]{:T(128)} %convert_element_type.93, () %tuple.26, (pred[128,512]{1,0:T(8,128)(4,1)}, bf16[2,512,8,128]{3,1,2,0:T(8,128)(2,1)}, bf16[8,2,128,128]{3,2,1,0:T(8,128)(2,1)}) %tuple.27), branch_computations={%region_4.0_spmd, %region_5.8_spmd} | conditional | flops 548669440 | bytes 27279448 | solution.py:148
  119.6 2.9 fusion
  125.6 2.9 fusion.9
  128.5 2.5 copy.136
  131.5 2.6 fusion.86
  134.1 50.1 %all-gather.11.cloned.1.call-done = bf16[1024,2048]{1,0:T(8,128)(2,1)} async-done(((bf16[32,2048]{1,0:T(8,128)(2,1)}), bf16[1024,2048]{1,0:T(8,128)(2,1)}) %all-gather.11.cloned.1.call-update) | async-done | bytes 4194320 | tf_op jit(solution)/shard_map/all_gather | solution.py:82
  184.2 3.9 multiply_reduce_fusion.6
  189.1 65.8 %all-gather.15.cloned.1.call-done = bf16[1024,3072]{1,0:T(8,128)(2,1)} async-done(((bf16[32,3072]{1,0:T(8,128)(2,1)}), bf16[1024,3072]{1,0:T(8,128)(2,1)}) %all-gather.15.cloned.1.call-update) | async-done | bytes 6291472 | tf_op jit(solution)/shard_map/all_gather | solution.py:160
  254.9 5.0 fusion.92
  259.8 65.5 %all-gather.13.cloned.1.call-done = bf16[1024,3072]{1,0:T(8,128)(2,1)} async-done(((bf16[32,3072]{1,0:T(8,128)(2,1)}), bf16[1024,3072]{1,0:T(8,128)(2,1)}) %all-gather.13.cloned.1.call-update) | async-done | bytes 6291472 | tf_op jit(solution)/shard_map/all_gather | solution.py:159
  325.3 4.9 fusion.91
  330.2 65.5 %all-gather.17.cloned.1.call-done = bf16[1024,3072]{1,0:T(8,128)(2,1)} async-done(((bf16[32,3072]{1,0:T(8,128)(2,1)}), bf16[1024,3072]{1,0:T(8,128)(2,1)}) %all-gather.17.cloned.1.call-update) | async-done | bytes 6291472 | tf_op jit(solution)/shard_map/all_gather | solution.py:161
  395.8 6.5 multiply_convert_fusion.1
  404.6 5.9 multiply_reduce_fusion.3
  413.1 2.2 reshape.242
  415.3 2.4 fusion.83
  417.7 14.5 %conditional.3 = (bf16[2,512,8,128]{3,1,2,0:T(8,128)(2,1)}, f32[8,2,128,128]{3,2,1,0:T(8,128)}) conditional(s32[]{:T(128)} %convert_element_type.93, () %tuple.28, (pred[128,512]{1,0:T(8,128)(4,1)}, bf16[2,512,8,128]{3,1,2,0:T(8,128)(2,1)}, bf16[8,2,128,128]{3,2,1,0:T(8,128)(2,1)}, f32[8,2,128]{2,1,0:T(2,128)}, f32[8,2,128]{2,1,0:T(2,128)}, ...), branch_computations={%region_10.11_spmd, %region_11.0_spmd} | conditional | flops 1355546624 | bytes 48685184 | solution.py:226
  417.7 2.6 copy.118
  441.4 20.6 %reduce-scatter.3.cloned.1.call-done = bf16[2,128,8,128]{3,1,2,0:T(8,128)(2,1)} async-done(((bf16[2,512,8,128]{3,1,2,0:T(8,128)(2,1)}), bf16[2,128,8,128]{3,1,2,0:T(8,128)(2,1)}) %reduce-scatter.3.cloned.1.call-update) | async-done | bytes 524304 | tf_op jit(solution)/shard_map/reduce_scatter | solution.py:229
  468.9 9.6 convolution_dynamic-update-slice_fusion
  478.5 4.6 convolution_dynamic-update-slice_fusion.3
  483.1 6.4 convolution_dynamic-update-slice_fusion.2
  489.5 6.6 convolution_dynamic-update-slice_fusion.1
  496.1 6.4 bitcast_dynamic-update-slice_fusion
  503.6 5.7 fusion.42
  509.3 6.8 fusion.57
  516.2 39.6 %all-reduce = (f32[1024]{0:T(1024)}, f32[1024]{0:T(1024)}, f32[128]{0:T(128)}, f32[128]{0:T(128)}) all-reduce(f32[1024]{0:T(1024)S(1)} %get-tuple-element.106, f32[1024]{0:T(1024)S(1)} %copy-done.37, f32[128]{0:T(128)S(1)} %bitcast_reduce_fusion, f32[128]{0:T(128)S(1)} %bitcast_reduce_fusion.1), channel_id=1, replica_groups=mesh['seq'=8,'ctx'=4] {'seq','ctx'}, use_global_device_ids=true, to_apply=%region_19.20 | all-reduce | flops 2304 | bytes 18432 | tf_op jit(solution)/shard_map/psum | solution.py:286
  556.7 463.5 %reduce-scatter.5.cloned.1.call-done = f32[32,15360]{1,0:T(8,128)} async-done(((f32[1024,15360]{1,0:T(8,128)}), f32[32,15360]{1,0:T(8,128)}) %reduce-scatter.5.cloned.1.call-update) | async-done | bytes 1966096 | tf_op jit(solution)/shard_map/reduce_scatter | solution.py:259
  1023.7 2.3 fusion.87
  (172 shorter events, 54.7 us)
Async XLA Ops:
  7.2 84.0 %all-gather.7.cloned.1.call-start = ((), (), s32[]{:S(2)}) async-start(), calls=%async_computation.2 | async-start | bytes 8650752 | tf_op jit(solution)/shard_map/all_gather | solution.py:81
  8.9 110.6 %all-gather.9.cloned.1.call-start = ((), (), s32[]{:S(2)}) async-start(), calls=%async_computation.3 | async-start | bytes 2621440 | tf_op jit(solution)/shard_map/all_gather | solution.py:130
  10.8 80.5 %copy-start.35 = (f32[128]{0:T(128)}, f32[128]{0:T(128)S(1)}, u32[]{:S(2)}) copy-start(f32[128]{0:T(128)S(1)} %add_rsqrt_fusion.3) | copy-start | bytes 1540
  96.2 6.6 copy-start.11
  97.2 6.3 copy-start.38
  98.2 86.0 %all-gather.11.cloned.1.call-start = ((), (), s32[]{:S(2)}) async-start(), calls=%async_computation.4 | async-start | bytes 4325376 | tf_op jit(solution)/shard_map/all_gather | solution.py:82
  99.0 155.9 %all-gather.15.cloned.1.call-start = ((), (), s32[]{:S(2)}) async-start(), calls=%async_computation.6 | async-start | bytes 6488064 | tf_op jit(solution)/shard_map/all_gather | solution.py:160
  99.5 225.8 %all-gather.13.cloned.1.call-start = ((), (), s32[]{:S(2)}) async-start(), calls=%async_computation.5 | async-start | bytes 6488064 | tf_op jit(solution)/shard_map/all_gather | solution.py:159
  100.1 295.6 %all-gather.17.cloned.1.call-start = ((), (), s32[]{:S(2)}) async-start(), calls=%async_computation.7 | async-start | bytes 6488064 | tf_op jit(solution)/shard_map/all_gather | solution.py:161
  100.7 361.3 %reduce-scatter.3.cloned.1.call-start = ((), (), s32[]{:S(2)}) async-start(), calls=%async_computation.8 | async-start | bytes 2621440 | tf_op jit(solution)/shard_map/reduce_scatter | solution.py:229
  119.6 64.6 %copy-start.8 = (bf16[1,128,1024]{2,1,0:T(8,128)(2,1)S(1)}, bf16[1,128,1024]{2,1,0:T(8,128)(2,1)}, u32[]{:S(2)}) copy-start(bf16[1,128,1024]{2,1,0:T(8,128)(2,1)} %param.18) | copy-start | bytes 786436
  131.5 57.5 %copy-start.33 = (f32[1024]{0:T(1024)S(1)}, f32[1024]{0:T(1024)}, u32[]{:S(2)}) copy-start(f32[1024]{0:T(1024)} %param.27) | copy-start | bytes 12292
  395.8 6.6 copy-start
  402.3 8.2 copy-start.15
  402.3 8.2 copy-start.17
  404.6 7.0 copy-start.1
  417.7 14.7 %copy-start.41 = (f32[128]{0:T(128)S(1)}, f32[128]{0:T(128)}, u32[]{:S(2)}) copy-start(f32[128]{0:T(128)} %param.25) | copy-start | bytes 1540
  417.7 15.3 %copy-start.39 = (f32[128]{0:T(128)S(1)}, f32[128]{0:T(128)}, u32[]{:S(2)}) copy-start(f32[128]{0:T(128)} %param.24) | copy-start | bytes 1540
  432.2 588.0 %reduce-scatter.5.cloned.1.call-start = ((), (), s32[]{:S(2)}) async-start(), calls=%async_computation.9 | async-start | bytes 64880640 | tf_op jit(solution)/shard_map/reduce_scatter | solution.py:259
  439.2 25.1 %copy-start.12 = (f32[16,8,8,128]{3,2,1,0:T(8,128)S(1)}, f32[16,8,8,128]{3,2,1,0:T(8,128)}, u32[]{:S(2)}) copy-start(f32[16,8,8,128]{3,2,1,0:T(8,128)} %copy-done.11) | copy-start | bytes 1572868
  468.9 9.6 copy-start.24
  468.9 9.6 copy-start.6
  468.9 9.6 copy-start.13
  483.1 6.4 copy-start.18
  489.5 6.6 copy-start.14
  489.5 6.6 copy-start.23
  502.6 6.7 copy-start.10
  502.6 6.7 copy-start.19
  502.6 6.7 copy-start.25
  502.6 6.7 copy-start.26
  502.6 6.7 copy-start.36
  509.3 6.8 copy-start.37
  (19 other events, 60.7 us)
Sparse Core Ops, SparseCore 0:
  11.4 79.7 all-gather.6
  98.3 21.1 all-gather.8
  122.4 61.7 all-gather.10
  186.9 67.9 all-gather.14
  257.6 67.6 all-gather.12
  328.0 67.6 all-gather.16
  432.3 29.6 reduce-scatter.2
  502.7 517.4 reduce-scatter.4
where the time goes:
time: 1040 us; the launch traced here: 1030 us
  waiting for transfers between devices  827 us (80%)
  matrix products  94.4 us (9%)
  blocking collectives  39.6 us (4%)
  other arithmetic  31.6 us (3%)
  local copies, waits for them, and re-layouts  23.6 us (2%)
  between operations  15.6 us (2%)
    reduce_scatter x1, waiting for transfers between devices, shards(): lax.psum_scatter(jnp.concatenate((jnp.concatenate((outer_rows(normed1, gr...  463 us
    all_gather x1, waiting for transfers between devices, shards(): lax.all_gather(w_joint, ('seq', 'ctx'), axis=0, tiled=True)  80.1 us
    all_gather x1, waiting for transfers between devices, shards(): lax.all_gather(w_up, ('seq', 'ctx'), axis=0, tiled=True)  65.8 us
    all_gather x1, waiting for transfers between devices, shards(): lax.all_gather(w_down, ('seq', 'ctx'), axis=0, tiled=True)  65.5 us
    all_gather x1, waiting for transfers between devices, shards(): lax.all_gather(w_gate, ('seq', 'ctx'), axis=0, tiled=True)  65.5 us
    all_gather x1, waiting for transfers between devices, shards(): lax.all_gather(w_out, ('seq', 'ctx'), axis=0, tiled=True)  50.1 us
    psum x1, blocking collectives, shards(): lax.psum((gain1_local, gain2_local, qgain_local, kgain_local), ('seq', 'c...  39.6 us
    dot_general x5, matrix products, outer_rows(): jnp.einsum('tj,tc->jc', left, right, preferred_element_type=jnp.float32)  33.6 us
  transfers between devices with their start and end apart: 8, of which 8 were waited for; matrix products, arithmetic and copies ran while one was open for 5% of the time, Pallas kernels for 0%

commit v1 on v0

--- a/solution.py
+++ b/solution.py
@@ -78,7 +78,12 @@
     normed1 = (unit1 * norm1_gain).astype(jnp.bfloat16)
     w_joint = jnp.concatenate((w_query, key_weight_matrix, value_weight_matrix), 1)
     joint_full, out_full = (
-        lax.all_gather(w_joint, ("seq", "ctx"), axis=0, tiled=True),
+        jnp.concatenate(
+            lax.all_to_all(
+                jnp.stack([w_joint] * lax.axis_size(("seq", "ctx"))), ("seq", "ctx"), 0, 0
+            ),
+            axis=0,
+        ),
         lax.all_gather(w_out, ("seq", "ctx"), axis=0, tiled=True),
     )
     projected_output = jnp.dot(normed1, joint_full, preferred_element_type=jnp.float32)

time: 1040 us -> 1160 us (1.12)
  waiting for transfers between devices: 827 us -> 930 us
    all_to_all x0 -> x1, waiting for transfers between devices: none -> 185 us  [shards(): lax.all_to_all(jnp.stack([w_joint] * lax.axis_size(('seq', 'ctx'))), ('se...]
    all_gather x1 -> x0, waiting for transfers between devices: 80.1 us -> none  [shards(): lax.all_gather(w_joint, ('seq', 'ctx'), axis=0, tiled=True)]
where the time goes in v1:
time: 1160 us; the launch traced here: 1150 us
  waiting for transfers between devices  930 us (80%)
  matrix products  94.3 us (8%)
  blocking collectives  39.6 us (3%)
  other arithmetic  30.9 us (3%)
  local copies, waits for them, and re-layouts  29.3 us (3%)
  between operations  15.8 us (1%)
    reduce_scatter x1, waiting for transfers between devices, shards(): lax.psum_scatter(jnp.concatenate((jnp.concatenate((outer_rows(normed1, gr...  464 us
    all_to_all x1, waiting for transfers between devices, shards(): lax.all_to_all(jnp.stack([w_joint] * lax.axis_size(('seq', 'ctx'))), ('se...  185 us
    all_gather x1, waiting for transfers between devices, shards(): lax.all_gather(w_up, ('seq', 'ctx'), axis=0, tiled=True)  66 us
    all_gather x1, waiting for transfers between devices, shards(): lax.all_gather(w_down, ('seq', 'ctx'), axis=0, tiled=True)  65.5 us
    all_gather x1, waiting for transfers between devices, shards(): lax.all_gather(w_gate, ('seq', 'ctx'), axis=0, tiled=True)  65.5 us
    all_gather x1, waiting for transfers between devices, shards(): lax.all_gather(w_out, ('seq', 'ctx'), axis=0, tiled=True)  50.3 us
    psum x1, blocking collectives, shards(): lax.psum((gain1_local, gain2_local, qgain_local, kgain_local), ('seq', 'c...  39.6 us
    dot_general x5, matrix products, outer_rows(): jnp.einsum('tj,tc->jc', left, right, preferred_element_type=jnp.float32)  33.6 us
  transfers between devices with their start and end apart: 8, of which 8 were waited for; matrix products, arithmetic and copies ran while one was open for 5% of the time, Pallas kernels for 0%

profile of v1, /device:TPU:0, one launch (start us, length us, event | category | flops | bytes accessed | tf_op | source)
XLA Modules:
  0.0 1148.2 jit_solution(535081191361211641)
XLA Ops:
  8.2 4.3 stack.10
  12.5 7.5 all-to-all-start
  20.5 185.3 %all-to-all-done = bf16[32,32,4096]{2,1,0:T(8,128)(2,1)} async-done(((bf16[32,32,4096]{2,1,0:T(8,128)(2,1)}), bf16[32,32,4096]{2,1,0:T(8,128)(2,1)}, u32[]{:S(2)}, u32[]{:S(2)}) %all-to-all-start) | async-done | bytes 8388640 | tf_op jit(solution)/shard_map/all_to_all | solution.py:82
  205.9 4.7 fusion.73
  223.4 10.8 all-gather.6.cloned.1.call-done
  234.2 11.6 %conditional.2 = (f32[8,2,128]{2,1,0:T(2,128)}, f32[8,2,128]{2,1,0:T(2,128)}, f32[8,2,128]{2,1,0:T(2,128)}, f32[8,2,128,128]{2,3,1,0:T(8,128)}) conditional(s32[]{:T(128)} %convert_element_type.101, () %tuple.26, (pred[128,512]{1,0:T(8,128)(4,1)}, bf16[2,512,8,128]{3,1,2,0:T(8,128)(2,1)}, bf16[8,2,128,128]{3,2,1,0:T(8,128)(2,1)}) %tuple.27), branch_computations={%region_4.0_spmd, %region_5.8_spmd} | conditional | flops 548669440 | bytes 27279448 | solution.py:153
  234.2 2.9 fusion
  240.2 2.9 fusion.9
  243.2 2.5 copy.136
  245.9 2.6 fusion.95
  248.5 50.3 %all-gather.8.cloned.1.call-done = bf16[1024,2048]{1,0:T(8,128)(2,1)} async-done(((bf16[32,2048]{1,0:T(8,128)(2,1)}), bf16[1024,2048]{1,0:T(8,128)(2,1)}) %all-gather.8.cloned.1.call-update) | async-done | bytes 4194320 | tf_op jit(solution)/shard_map/all_gather | solution.py:87
  298.9 3.9 multiply_reduce_fusion.6
  303.7 66.0 %all-gather.12.cloned.1.call-done = bf16[1024,3072]{1,0:T(8,128)(2,1)} async-done(((bf16[32,3072]{1,0:T(8,128)(2,1)}), bf16[1024,3072]{1,0:T(8,128)(2,1)}) %all-gather.12.cloned.1.call-update) | async-done | bytes 6291472 | tf_op jit(solution)/shard_map/all_gather | solution.py:165
  369.7 5.0 fusion.101
  374.7 65.5 %all-gather.10.cloned.1.call-done = bf16[1024,3072]{1,0:T(8,128)(2,1)} async-done(((bf16[32,3072]{1,0:T(8,128)(2,1)}), bf16[1024,3072]{1,0:T(8,128)(2,1)}) %all-gather.10.cloned.1.call-update) | async-done | bytes 6291472 | tf_op jit(solution)/shard_map/all_gather | solution.py:164
  440.1 4.9 fusion.100
  445.1 65.5 %all-gather.14.cloned.1.call-done = bf16[1024,3072]{1,0:T(8,128)(2,1)} async-done(((bf16[32,3072]{1,0:T(8,128)(2,1)}), bf16[1024,3072]{1,0:T(8,128)(2,1)}) %all-gather.14.cloned.1.call-update) | async-done | bytes 6291472 | tf_op jit(solution)/shard_map/all_gather | solution.py:166
  510.6 6.5 multiply_convert_fusion.1
  519.4 5.9 multiply_reduce_fusion.3
  530.1 2.4 fusion.92
  532.5 14.4 %conditional.3 = (bf16[2,512,8,128]{3,1,2,0:T(8,128)(2,1)}, f32[8,2,128,128]{3,2,1,0:T(8,128)}) conditional(s32[]{:T(128)} %convert_element_type.101, () %tuple.28, (pred[128,512]{1,0:T(8,128)(4,1)}, bf16[2,512,8,128]{3,1,2,0:T(8,128)(2,1)}, bf16[8,2,128,128]{3,2,1,0:T(8,128)(2,1)}, f32[8,2,128]{2,1,0:T(2,128)}, f32[8,2,128]{2,1,0:T(2,128)}, ...), branch_computations={%region_10.11_spmd, %region_11.0_spmd} | conditional | flops 1355546624 | bytes 48685184 | solution.py:231
  532.5 2.6 copy.118
  556.2 20.6 %reduce-scatter.3.cloned.1.call-done = bf16[2,128,8,128]{3,1,2,0:T(8,128)(2,1)} async-done(((bf16[2,512,8,128]{3,1,2,0:T(8,128)(2,1)}), bf16[2,128,8,128]{3,1,2,0:T(8,128)(2,1)}) %reduce-scatter.3.cloned.1.call-update) | async-done | bytes 524304 | tf_op jit(solution)/shard_map/reduce_scatter | solution.py:234
  583.7 9.6 convolution_dynamic-update-slice_fusion
  593.3 4.6 convolution_dynamic-update-slice_fusion.3
  597.9 6.4 convolution_dynamic-update-slice_fusion.2
  604.3 6.7 convolution_dynamic-update-slice_fusion.1
  611.0 6.4 bitcast_dynamic-update-slice_fusion
  618.4 5.7 fusion.42
  624.2 6.8 fusion.59
  631.0 39.6 %all-reduce = (f32[1024]{0:T(1024)}, f32[1024]{0:T(1024)}, f32[128]{0:T(128)}, f32[128]{0:T(128)}) all-reduce(f32[1024]{0:T(1024)S(1)} %get-tuple-element.106, f32[1024]{0:T(1024)S(1)} %copy-done.37, f32[128]{0:T(128)S(1)} %bitcast_reduce_fusion, f32[128]{0:T(128)S(1)} %bitcast_reduce_fusion.1), channel_id=1, replica_groups=mesh['seq'=8,'ctx'=4] {'seq','ctx'}, use_global_device_ids=true, to_apply=%region_19.20 | all-reduce | flops 2304 | bytes 18432 | tf_op jit(solution)/shard_map/psum | solution.py:291
  671.6 463.5 %reduce-scatter.5.cloned.1.call-done = f32[32,15360]{1,0:T(8,128)} async-done(((f32[1024,15360]{1,0:T(8,128)}), f32[32,15360]{1,0:T(8,128)}) %reduce-scatter.5.cloned.1.call-update) | async-done | bytes 1966096 | tf_op jit(solution)/shard_map/reduce_scatter | solution.py:264
  (174 shorter events, 60.1 us)
Async XLA Ops:
  12.5 7.5 copy-start.8
  12.5 7.7 copy-start.43
  12.5 193.4 %copy-start.32 = (f32[1024]{0:T(1024)S(1)}, f32[1024]{0:T(1024)}, u32[]{:S(2)}) copy-start(f32[1024]{0:T(1024)} %param.20) | copy-start | bytes 12292
  12.5 193.4 %all-to-all-start = ((bf16[32,32,4096]{2,1,0:T(8,128)(2,1)}), bf16[32,32,4096]{2,1,0:T(8,128)(2,1)}, u32[]{:S(2)}, u32[]{:S(2)}) async-start(bf16[32,32,4096]{2,1,0:T(8,128)(2,1)} %stack.10), calls=%async_computation | async-start | bytes 16777216 | tf_op jit(solution)/shard_map/all_to_all | solution.py:82
  20.0 214.3 %all-gather.6.cloned.1.call-start = ((), (), s32[]{:S(2)}) async-start(), calls=%async_computation.3 | async-start | bytes 2621440 | tf_op jit(solution)/shard_map/all_gather | solution.py:135
  20.2 190.4 %copy-start.35 = (f32[128]{0:T(128)}, f32[128]{0:T(128)S(1)}, u32[]{:S(2)}) copy-start(f32[128]{0:T(128)S(1)} %add_rsqrt_fusion.3) | copy-start | bytes 1540
  210.8 9.1 copy-start.11
  212.5 8.7 copy-start.38
  214.5 84.4 %all-gather.8.cloned.1.call-start = ((), (), s32[]{:S(2)}) async-start(), calls=%async_computation.4 | async-start | bytes 4325376 | tf_op jit(solution)/shard_map/all_gather | solution.py:87
  215.2 154.5 %all-gather.12.cloned.1.call-start = ((), (), s32[]{:S(2)}) async-start(), calls=%async_computation.6 | async-start | bytes 6488064 | tf_op jit(solution)/shard_map/all_gather | solution.py:165
  216.0 224.2 %all-gather.10.cloned.1.call-start = ((), (), s32[]{:S(2)}) async-start(), calls=%async_computation.5 | async-start | bytes 6488064 | tf_op jit(solution)/shard_map/all_gather | solution.py:164
  216.5 294.0 %all-gather.14.cloned.1.call-start = ((), (), s32[]{:S(2)}) async-start(), calls=%async_computation.7 | async-start | bytes 6488064 | tf_op jit(solution)/shard_map/all_gather | solution.py:166
  217.1 359.7 %reduce-scatter.3.cloned.1.call-start = ((), (), s32[]{:S(2)}) async-start(), calls=%async_computation.8 | async-start | bytes 2621440 | tf_op jit(solution)/shard_map/reduce_scatter | solution.py:234
  245.9 57.7 %copy-start.33 = (f32[1024]{0:T(1024)S(1)}, f32[1024]{0:T(1024)}, u32[]{:S(2)}) copy-start(f32[1024]{0:T(1024)} %param.27) | copy-start | bytes 12292
  510.6 6.6 copy-start
  517.1 8.2 copy-start.15
  517.1 8.2 copy-start.17
  519.4 7.0 copy-start.1
  532.5 14.7 %copy-start.40 = (f32[128]{0:T(128)S(1)}, f32[128]{0:T(128)}, u32[]{:S(2)}) copy-start(f32[128]{0:T(128)} %param.25) | copy-start | bytes 1540
  547.0 588.1 %reduce-scatter.5.cloned.1.call-start = ((), (), s32[]{:S(2)}) async-start(), calls=%async_computation.9 | async-start | bytes 64880640 | tf_op jit(solution)/shard_map/reduce_scatter | solution.py:264
  554.1 25.1 %copy-start.12 = (f32[16,8,8,128]{3,2,1,0:T(8,128)S(1)}, f32[16,8,8,128]{3,2,1,0:T(8,128)}, u32[]{:S(2)}) copy-start(f32[16,8,8,128]{3,2,1,0:T(8,128)} %copy-done.11) | copy-start | bytes 1572868
  583.7 9.6 copy-start.24
  583.7 9.6 copy-start.6
  583.7 9.6 copy-start.13
  604.3 6.7 copy-start.14
  604.3 6.7 copy-start.23
  617.4 6.7 copy-start.10
  617.4 6.7 copy-start.19
  617.4 6.7 copy-start.25
  617.4 6.7 copy-start.26
  617.5 6.7 copy-start.36
  624.2 6.9 copy-start.37
  (20 other events, 59.2 us)
Sparse Core Ops, SparseCore 0:
  214.6 19.5 all-gather.5
  237.1 61.7 all-gather.7
  301.7 67.9 all-gather.11
  372.4 67.6 all-gather.9
  442.9 67.6 all-gather.13
  547.1 29.6 reduce-scatter.2
  617.5 517.5 reduce-scatter.4
